TPU v7x, 128 devices: a whole 4x4x4 slice. The times are simulated.
128 devices in a mesh: req: 32 (over z, y, x_lo), exp: 4 (over x_hi, core).
Axes of the slice: x: 4 (x_hi: 2, x_lo: 2; x = x_hi * 2 + x_lo), y: 4, z: 4, core: 2. Of those that a mesh axis runs over, the one named last changes fastest.
Arguments:
- hidden_in: bfloat16 [8192, 2048], P(('req', 'exp')), may hold values from -6 to 6
- query_in: bfloat16 [8192, 2048], P('req', 'exp'), may hold values from -6 to 6
- key_in: bfloat16 [8192, 2048], P('req', 'exp'), may hold values from -6 to 6
- value_in: bfloat16 [8192, 2048], P('req', 'exp'), may hold values from -24 to 24
- query_gain: float32 [128], replicated, may hold values from 0.5 to 2.5
- key_gain: float32 [128], replicated, may hold values from 0.5 to 2.5
- cache_keys: bfloat16 [64, 32, 2048], P('req', None, 'exp'), may hold values from -400 to 400
- cache_values: bfloat16 [64, 32, 2048], P('req', None, 'exp'), may hold values from -24 to 24
- cache_block: int32 [128], replicated, may hold values from -1 to 63, as said below
- request_lengths: int32 [32, 4], P('req'), may hold values from 1 to 128, 256 in all within a row
- out_proj: bfloat16 [2048, 2048], P('exp'), may hold values from -0.125 to 0.125
- norm_gain: float32 [2048], replicated, may hold values from 0.25 to 1.75
- expert_ids: int32 [8192, 8], P(('req', 'exp')), may hold values from 0 to 63, all different within a row; in each aligned block of 64 rows (0 to 63, 64 to 127, ...) at most 10 rows name the same one
- gate_values: float32 [8192, 8], P(('req', 'exp')), may hold values from 0.4 to 1.6
- old_slots: int32 [64], replicated, may hold values from 0 to 63, each once
- new_replicas: int32 [32], replicated, may hold values from 0 to 63
- slot_weights: bfloat16 [64, 3, 2048, 1024], P('req', None, None, 'exp'), may hold values from -0.125 to 0.125
Outputs:
- layer_out: bfloat16 [8192, 2048], P(('req', 'exp'))
- replica_weights: bfloat16 [32, 3, 2048, 1024], P('req', None, None, 'exp')
Inputs may be any that keep to these rules, and one draw needn't show every extreme that they name: `cache_block`: each index of req has exactly 2 of its 4 requests with a block; every block serves exactly one request. `expert_ids`: in each aligned block of 64 rows (the rows of one device) no expert is named by more than 10 rows, a bound that some block reaches; the 8 experts of a row differ. `old_slots`: every expert is in exactly one slot. `request_lengths`: the lengths of each index of req sum to 256.
All inputs are finite; a program needn't handle non-finite values.
Results may differ from a plain program's by a relative error of at most 0.025.
Values may be sent and summed in bfloat16 or wider, within the bound.
A program may use at most 128 MiB of HBM per device.

v0:
```python
import math
import jax
import jax.numpy as jnp
from jax import lax
from jax.sharding import PartitionSpec as P


def prepare(values, gain, position):
    vector = values.astype(jnp.float32)
    scaled = vector * lax.rsqrt(jnp.mean(vector * vector, axis=-1, keepdims=True) + 1e-06) * gain
    half_size = scaled.shape[-1] // 2
    frequency = 10000.0 ** (-(jnp.arange(half_size, dtype=jnp.float32) * 2.0 / scaled.shape[-1]))
    angles = position[:, None] * frequency[None, :]
    cosine = jnp.cos(angles)[:, None, :]
    sine_part = jnp.sin(angles)[:, None, :]
    lower_half = scaled[..., :half_size]
    upper_half = scaled[..., half_size:]
    rotated = jnp.concatenate(
        [
            lower_half * cosine - upper_half * sine_part,
            upper_half * cosine + lower_half * sine_part,
        ],
        axis=-1,
    )
    return rotated.astype(jnp.bfloat16)


def compact(block_rows, slots_wanted):
    live = block_rows >= 0
    ranks = jnp.cumsum(live.astype(jnp.int32), axis=1) - 1
    request_idx = jnp.arange(block_rows.shape[1], dtype=jnp.int32)[None, :]
    chosen_blocks = []
    chosen_requests = []
    for slot_num in range(slots_wanted):
        picked = live & (ranks == slot_num)
        chosen_blocks.append(jnp.sum(jnp.where(picked, block_rows, 0), axis=1))
        chosen_requests.append(jnp.sum(jnp.where(picked, request_idx, 0), axis=1))
    return (jnp.stack(chosen_blocks, axis=1), jnp.stack(chosen_requests, axis=1))


def run_slots(inbox, slot_weights, capacity):
    sources = inbox.shape[0]
    model_width = inbox.shape[2]
    slot_count = slot_weights.shape[0]
    grouped = inbox.reshape(sources, slot_count, capacity, model_width)
    results = []
    for slot_num in range(slot_count):
        in_rows = grouped[:, slot_num].reshape(sources * capacity, model_width)
        gate_act = jnp.dot(in_rows, slot_weights[slot_num, 0], preferred_element_type=jnp.float32)
        up_act = jnp.dot(in_rows, slot_weights[slot_num, 1], preferred_element_type=jnp.float32)
        hidden = (jax.nn.silu(gate_act) * up_act).astype(jnp.bfloat16)
        partial_value = lax.dot_general(
            hidden,
            slot_weights[slot_num, 2],
            (((1,), (1,)), ((), ())),
            preferred_element_type=jnp.float32,
        )
        results.append(partial_value.reshape(sources, capacity, model_width))
    return jnp.stack(results, axis=1).reshape(sources, slot_count * capacity, model_width)


def body(
    hidden_in,
    query_in,
    key_in,
    value_in,
    query_gain,
    key_gain,
    cache_keys,
    cache_values,
    cache_block,
    request_lengths,
    out_proj,
    norm_gain,
    expert_ids,
    gate_values,
    old_slots,
    new_replicas,
    slot_weights,
):
    req_count = lax.axis_size("req")
    exp_count = lax.axis_size("exp")
    group_idx = lax.axis_index("req")
    tok_grp, width_q = query_in.shape
    tok_dev, model_width = hidden_in.shape
    head_size = query_gain.shape[0]
    head_count = width_q // head_size
    cache_dev = cache_keys.shape[0]
    pre_len = cache_keys.shape[1]
    req_grp = request_lengths.shape[1]
    lengths = request_lengths[0]
    req_ends = jnp.cumsum(lengths)
    starts = req_ends - lengths
    places = jnp.arange(tok_grp, dtype=jnp.int32)
    member = (places[:, None] >= starts[None, :]) & (places[:, None] < req_ends[None, :])
    request_idx = jnp.arange(req_grp, dtype=jnp.int32)
    segment = jnp.sum(jnp.where(member, request_idx[None, :], 0), axis=1)
    offset = places - jnp.sum(jnp.where(member, starts[None, :], 0), axis=1)
    block_rows = cache_block.reshape(req_count, req_grp)
    my_blocks = lax.dynamic_index_in_dim(block_rows, group_idx, 0, keepdims=False)
    has_cache = my_blocks >= 0
    token_cached = jnp.sum(jnp.where(member & has_cache[None, :], 1, 0), axis=1) > 0
    position = (offset + jnp.where(token_cached, pre_len, 0)).astype(jnp.float32)
    need_blocks, need_requests = compact(block_rows, cache_dev)
    my_requests = lax.dynamic_index_in_dim(need_requests, group_idx, 0, keepdims=False)
    every_keys, every_values = (
        lax.all_gather(cache_keys, "req", axis=0, tiled=True),
        lax.all_gather(cache_values, "req", axis=0, tiled=True),
    )
    wanted = lax.dynamic_index_in_dim(need_blocks, group_idx, 0, keepdims=False)
    far_keys = jnp.take(every_keys, wanted, axis=0)
    far_values = jnp.take(every_values, wanted, axis=0)
    query_n = prepare(query_in.reshape(tok_grp, head_count, head_size), query_gain, position)
    key_n = prepare(key_in.reshape(tok_grp, head_count, head_size), key_gain, position)
    keyset = jnp.concatenate(
        [key_n, far_keys.reshape(cache_dev * pre_len, head_count, head_size)], axis=0
    )
    valueset = jnp.concatenate(
        [
            value_in.reshape(tok_grp, head_count, head_size),
            far_values.reshape(cache_dev * pre_len, head_count, head_size),
        ],
        axis=0,
    )
    key_request = jnp.concatenate([segment, jnp.repeat(my_requests, pre_len)])
    allowed = segment[:, None] == key_request[None, :]
    scores = jnp.einsum("qhd,khd->hqk", query_n, keyset, preferred_element_type=jnp.float32) * (
        1.0 / math.sqrt(head_size)
    )
    scores = jnp.where(allowed[None], scores, -1e30)
    peak = jnp.max(scores, axis=-1, keepdims=True)
    expos = jnp.exp(scores - peak)
    weights = (expos / jnp.sum(expos, axis=-1, keepdims=True)).astype(jnp.bfloat16)
    attended = jnp.einsum("hqk,khd->qhd", weights, valueset, preferred_element_type=jnp.float32)
    attended = attended.astype(jnp.bfloat16).reshape(tok_grp, width_q)
    attn_out = lax.psum_scatter(
        jnp.dot(attended, out_proj, preferred_element_type=jnp.float32),
        "exp",
        scatter_dimension=0,
        tiled=True,
    )
    residual = hidden_in.astype(jnp.float32) + attn_out
    normed = (
        residual
        * lax.rsqrt(jnp.mean(residual * residual, axis=-1, keepdims=True) + 1e-06)
        * norm_gain
    ).astype(jnp.bfloat16)
    topk_count = expert_ids.shape[1]
    slot_total = old_slots.shape[0]
    slots_here = slot_weights.shape[0]
    capacity = max(2, tok_dev * topk_count * 5 // (4 * slot_total))
    slot_range = jnp.arange(slot_total, dtype=jnp.int32)
    slot_of = jnp.sum(
        jnp.where(old_slots[None, :] == slot_range[:, None], slot_range[None, :], 0), axis=1
    )
    flat_ids = expert_ids.reshape(-1)
    onehot = flat_ids[:, None] == slot_range[None, :]
    row_slot = jnp.sum(jnp.where(onehot, slot_of[None, :], 0), axis=1)
    before = jnp.cumsum(onehot.astype(jnp.int32), axis=0) - onehot.astype(jnp.int32)
    row_rank = jnp.sum(jnp.where(onehot, before, 0), axis=1)
    target = row_slot * capacity + row_rank
    send_rows = jnp.repeat(normed, topk_count, axis=0)
    outbox = jnp.zeros((slot_total * capacity, model_width), jnp.bfloat16).at[target].set(send_rows)
    outbox = outbox.reshape(req_count, slots_here * capacity, model_width)
    copies = jnp.broadcast_to(
        outbox[:, None], (req_count, exp_count, slots_here * capacity, model_width)
    )
    copies = copies.reshape(req_count * exp_count, slots_here * capacity, model_width)
    inbox = lax.all_to_all(copies, ("req", "exp"), split_axis=0, concat_axis=0, tiled=True)
    partial_value = run_slots(inbox, slot_weights, capacity).astype(jnp.bfloat16)
    returned = lax.all_to_all(
        partial_value, ("req", "exp"), split_axis=0, concat_axis=0, tiled=True
    )
    result = jnp.sum(
        returned.astype(jnp.float32).reshape(
            req_count, exp_count, slots_here * capacity, model_width
        ),
        axis=1,
    )
    result_rows = jnp.take(result.reshape(slot_total * capacity, model_width), target, axis=0)
    mixture = jnp.sum(
        result_rows.reshape(tok_dev, topk_count, model_width) * gate_values[:, :, None], axis=1
    )
    layer_out = (residual + mixture).astype(jnp.bfloat16)
    spread_slots = lax.all_to_all(slot_weights, "req", split_axis=2, concat_axis=0, tiled=True)
    replica_onehot = new_replicas[:, None] == slot_range[None, :]
    source_slot = jnp.sum(jnp.where(replica_onehot, slot_of[None, :], 0), axis=1)
    chosen_pieces = jnp.take(spread_slots, source_slot, axis=0)
    replica_weights = lax.all_to_all(chosen_pieces, "req", split_axis=0, concat_axis=2, tiled=True)
    return (layer_out, replica_weights)


def solution(mesh):
    in_specs = (
        P(("req", "exp"), None),
        P("req", "exp"),
        P("req", "exp"),
        P("req", "exp"),
        P(),
        P(),
        P("req", None, "exp"),
        P("req", None, "exp"),
        P(),
        P("req", None),
        P("exp", None),
        P(),
        P(("req", "exp"), None),
        P(("req", "exp"), None),
        P(),
        P(),
        P("req", None, None, "exp"),
    )
    out_specs = (P(("req", "exp"), None), P("req", None, None, "exp"))
    return jax.shard_map(body, mesh=mesh, in_specs=in_specs, out_specs=out_specs, check_vma=False)
```

profile of v0, /device:TPU:74, one launch (start us, length us, event | category | flops | bytes accessed | tf_op | source)
XLA Modules:
  0.0 917.7 jit_solution(13939975030181986648)
XLA Ops:
  8.7 10.5 %copy.102 = bf16[2,3,2048,256]{3,1,0,2:T(4,128)(2,1)} copy(bf16[2,3,2048,256]{3,2,1,0:T(8,128)(2,1)} %param.35) | data formatting | bytes 12582912 | tf_op args[16]
  19.2 8.7 all-to-all-start.2
  36.1 141.0 %all-gather.3.cloned.1.call-done = bf16[64,32,512]{2,1,0:T(8,128)(2,1)} async-done(((bf16[2,32,512]{2,1,0:T(8,128)(2,1)}), bf16[64,32,512]{2,1,0:T(8,128)(2,1)}) %all-gather.3.cloned.1.call-update) | async-done | bytes 2097168 | tf_op jit(solution)/shard_map/all_gather | solution.py:108
  179.2 152.2 %all-gather.5.cloned.1.call-done = bf16[64,32,512]{2,1,0:T(8,128)(2,1)} async-done(((bf16[2,32,512]{2,1,0:T(8,128)(2,1)}), bf16[64,32,512]{2,1,0:T(8,128)(2,1)}) %all-gather.5.cloned.1.call-update) | async-done | bytes 2097168 | tf_op jit(solution)/shard_map/all_gather | solution.py:107
  342.3 52.4 %reduce-scatter.2.cloned.1.call-done = f32[64,2048]{1,0:T(8,128)} async-done(((f32[256,2048]{1,0:T(8,128)}), f32[64,2048]{1,0:T(8,128)}) %reduce-scatter.2.cloned.1.call-update) | async-done | bytes 524304 | tf_op jit(solution)/shard_map/reduce_scatter | solution.py:136
  397.1 5.6 scatter_custom_fusion
  407.8 8.1 broadcast_in_dim.196
  416.0 9.2 %all-to-all-start = ((bf16[128,20,2048]{2,1,0:T(8,128)(2,1)}), bf16[128,20,2048]{2,1,0:T(8,128)(2,1)}, u32[]{:S(2)}, u32[]{:S(2)}) async-start(bf16[128,20,2048]{2,1,0:T(8,128)(2,1)} %bitcast.108), calls=%async_computation.1 | async-start | bytes 25165824 | tf_op jit(solution)/shard_map/all_to_all | solution.py:169
  433.6 5.2 gather_fusion.1
  442.7 145.0 %all-to-all-done = bf16[128,20,2048]{2,1,0:T(8,128)(2,1)} async-done(((bf16[128,20,2048]{2,1,0:T(8,128)(2,1)}), bf16[128,20,2048]{2,1,0:T(8,128)(2,1)}, u32[]{:S(2)}, u32[]{:S(2)}) %all-to-all-start) | async-done | bytes 10485792 | tf_op jit(solution)/shard_map/all_to_all | solution.py:169
  587.7 6.8 all-to-all-start.3
  594.5 12.6 %copy.93 = bf16[128,20,2048]{2,0,1:T(8,128)(2,1)} copy(bf16[128,20,2048]{2,1,0:T(8,128)(2,1)} %all-to-all-done) | data formatting | bytes 20971520 | tf_op jit(solution)/shard_map/all_to_all | solution.py:169
  607.2 10.2 %fusion.64 = (bf16[128,1,10,2048]{3,0,2,1:T(8,128)(2,1)}, bf16[128,1,10,2048]{3,0,2,1:T(8,128)(2,1)}) fusion(bf16[128,2,10,2048]{3,0,2,1:T(8,128)(2,1)} %bitcast.109), kind=kLoop, calls=%fused_computation.135 | loop fusion | bytes 20971520 | tf_op jit(solution)/shard_map/slice | solution.py:48
  617.3 9.0 copy.94
  626.4 10.0 %reshape_squeeze.6 = bf16[1280,2048]{1,0:T(8,128)(2,1)} reshape(bf16[128,1,10,2048]{3,2,0,1:T(8,128)(2,1)} %copy.94) | data formatting | bytes 10485760 | tf_op jit(solution)/shard_map/reshape;squeeze | solution.py:48
  644.1 9.0 copy.96
  653.1 10.2 %reshape_squeeze.7 = bf16[1280,2048]{1,0:T(8,128)(2,1)} reshape(bf16[128,1,10,2048]{3,2,0,1:T(8,128)(2,1)} %copy.96) | data formatting | bytes 10485760 | tf_op jit(solution)/shard_map/reshape;squeeze | solution.py:48
  681.2 9.0 pad_maximum_fusion
  690.1 14.1 %copy.98 = bf16[128,20,2048]{2,1,0:T(8,128)(2,1)} copy(bf16[128,20,2048]{2,0,1:T(8,128)(2,1)} %bitcast.110) | data formatting | bytes 20971520 | tf_op jit(solution)/shard_map/convert_element_type | solution.py:170
  704.2 10.9 %all-to-all-start.1 = ((bf16[128,20,2048]{2,1,0:T(8,128)(2,1)}), bf16[128,20,2048]{2,1,0:T(8,128)(2,1)}, u32[]{:S(2)}, u32[]{:S(2)}) async-start(bf16[128,20,2048]{2,1,0:T(8,128)(2,1)} %copy.98), calls=%async_computation.2 | async-start | bytes 25165824 | tf_op jit(solution)/shard_map/all_to_all | solution.py:171
  719.3 160.7 %all-to-all-done.1 = bf16[128,20,2048]{2,1,0:T(8,128)(2,1)} async-done(((bf16[128,20,2048]{2,1,0:T(8,128)(2,1)}), bf16[128,20,2048]{2,1,0:T(8,128)(2,1)}, u32[]{:S(2)}, u32[]{:S(2)}) %all-to-all-start.1) | async-done | bytes 10485792 | tf_op jit(solution)/shard_map/all_to_all | solution.py:171
  880.0 11.1 %convert_reduce_fusion = f32[32,20,2048]{2,1,0:T(8,128)} fusion(bf16[128,20,2048]{2,1,0:T(8,128)(2,1)} %all-to-all-done.1), kind=kLoop, calls=%fused_computation.6 | loop fusion | flops 9175040 | bytes 15728640 | tf_op jit(solution)/shard_map/reduce_sum | solution.py:174
  891.2 6.8 reshape.297
  898.0 8.1 gather_fusion
  (127 shorter events, 76.6 us)
Async XLA Ops:
  7.2 331.0 %copy-start = (bf16[512,2048]{1,0:T(8,128)(2,1)S(1)}, bf16[512,2048]{1,0:T(8,128)(2,1)}, u32[]{:S(2)}) copy-start(bf16[512,2048]{1,0:T(8,128)(2,1)} %param.29) | copy-start | bytes 6291460
  7.2 169.9 %all-gather.3.cloned.1.call-start = ((), (), s32[]{:S(2)}) async-start(), calls=%async_computation.5 | async-start | bytes 2162688 | tf_op jit(solution)/shard_map/all_gather | solution.py:108
  7.9 323.5 %all-gather.5.cloned.1.call-start = ((), (), s32[]{:S(2)}) async-start(), calls=%async_computation.6 | async-start | bytes 2162688 | tf_op jit(solution)/shard_map/all_gather | solution.py:107
  19.1 8.9 copy-start.12
  19.1 9.9 %copy-start.15 = (s32[1,4]{1,0:T(1,128)S(1)}, s32[1,4]{1,0:T(1,128)}, u32[]{:S(2)}) copy-start(s32[1,4]{1,0:T(1,128)} %param.28) | copy-start | bytes 52
  19.2 10.1 %copy-start.6 = (bf16[256,512]{1,0:T(8,128)(2,1)S(1)}, bf16[256,512]{1,0:T(8,128)(2,1)}, u32[]{:S(2)}) copy-start(bf16[256,512]{1,0:T(8,128)(2,1)} %param.20) | copy-start | bytes 786436
  19.2 10.3 %copy-start.7 = (bf16[256,512]{1,0:T(8,128)(2,1)S(1)}, bf16[256,512]{1,0:T(8,128)(2,1)}, u32[]{:S(2)}) copy-start(bf16[256,512]{1,0:T(8,128)(2,1)} %param.21) | copy-start | bytes 786436
  19.2 388.7 %all-to-all-start.2 = ((bf16[2,3,2048,256]{3,1,0,2:T(4,128)(2,1)}), bf16[2,3,2048,256]{3,1,0,2:T(4,128)(2,1)}, u32[]{:S(2)}, u32[]{:S(2)}) async-start(bf16[2,3,2048,256]{3,1,0,2:T(4,128)(2,1)} %copy.102), calls=%async_computation.3 | async-start | bytes 16777216 | tf_op jit(solution)/shard_map/all_to_all | solution.py:185
  27.9 5.6 copy-start.13
  27.9 5.6 copy-start.14
  27.9 366.8 %reduce-scatter.2.cloned.1.call-start = ((), (), s32[]{:S(2)}) async-start(), calls=%async_computation.7 | async-start | bytes 2621440 | tf_op jit(solution)/shard_map/reduce_scatter | solution.py:136
  34.9 301.6 %copy-start.8 = (bf16[256,4,128]{2,0,1:T(8,128)(2,1)S(1)}, bf16[256,4,128]{2,0,1:T(8,128)(2,1)}, u32[]{:S(2)}) copy-start(bf16[256,4,128]{2,0,1:T(8,128)(2,1)} %copy.83) | copy-start | bytes 786436
  338.2 3.9 copy-start.16
  338.2 56.6 %copy-start.5 = (bf16[64,2048]{1,0:T(8,128)(2,1)S(1)}, bf16[64,2048]{1,0:T(8,128)(2,1)}, u32[]{:S(2)}) copy-start(bf16[64,2048]{1,0:T(8,128)(2,1)} %param.19) | copy-start | bytes 786436
  338.2 57.8 %copy-start.9 = (f32[2048]{0:T(1024)S(1)}, f32[2048]{0:T(1024)}, u32[]{:S(2)}) copy-start(f32[2048]{0:T(1024)} %param.30) | copy-start | bytes 24580
  416.0 9.2 %copy-start.17 = (s32[32]{0:T(128)S(1)}, s32[32]{0:T(128)}, u32[]{:S(2)}) copy-start(s32[32]{0:T(128)} %param.34) | copy-start | bytes 388
  416.0 171.7 %all-to-all-start = ((bf16[128,20,2048]{2,1,0:T(8,128)(2,1)}), bf16[128,20,2048]{2,1,0:T(8,128)(2,1)}, u32[]{:S(2)}, u32[]{:S(2)}) async-start(bf16[128,20,2048]{2,1,0:T(8,128)(2,1)} %bitcast.108), calls=%async_computation.1 | async-start | bytes 25165824 | tf_op jit(solution)/shard_map/all_to_all | solution.py:169
  587.7 116.5 %all-to-all-start.3 = ((bf16[32,3,64,256]{3,2,1,0:T(8,128)(2,1)}), bf16[32,3,64,256]{3,2,1,0:T(8,128)(2,1)}, u32[]{:S(2)}, u32[]{:S(2)}) async-start(bf16[32,3,64,256]{3,2,1,0:T(8,128)(2,1)} %broadcast_select_fusion), calls=%async_computation.4 | async-start | bytes 6291456 | tf_op jit(solution)/shard_map/all_to_all | solution.py:189
  636.4 4.5 copy-start.2
  663.3 4.5 copy-start.3
  704.2 11.0 %copy-start.11 = (f32[64,8]{0,1:T(8,128)S(1)}, f32[64,8]{0,1:T(8,128)}, u32[]{:S(2)}) copy-start(f32[64,8]{0,1:T(8,128)} %param.32) | copy-start | bytes 6148
  704.2 175.8 %all-to-all-start.1 = ((bf16[128,20,2048]{2,1,0:T(8,128)(2,1)}), bf16[128,20,2048]{2,1,0:T(8,128)(2,1)}, u32[]{:S(2)}, u32[]{:S(2)}) async-start(bf16[128,20,2048]{2,1,0:T(8,128)(2,1)} %copy.98), calls=%async_computation.2 | async-start | bytes 25165824 | tf_op jit(solution)/shard_map/all_to_all | solution.py:171
  898.0 13.0 %copy-start.1 = (bf16[512,2048]{1,0:T(8,128)(2,1)S(1)}, bf16[512,2048]{1,0:T(8,128)(2,1)}, u32[]{:S(2)}) copy-start(bf16[512,2048]{1,0:T(8,128)(2,1)} %param.29) | copy-start | bytes 6291460
  906.1 4.1 copy-start.4
  (1 other events, 2.1 us)
Sparse Core Ops, SparseCore 0:
  9.7 167.3 all-gather.2
  178.7 152.7 all-gather.4
  340.4 54.2 reduce-scatter.1
where the time goes:
time: 928 us; the launch traced here: 918 us
  waiting for transfers between devices  653 us (70%)
  local copies, waits for them, and re-layouts  146 us (16%)
  other arithmetic  37.1 us (4%)
  starting transfers between devices  35.8 us (4%)
  matrix products  31.5 us (3%)
  between operations  14.5 us (2%)
    all_to_all x1, waiting for transfers between devices, body(): lax.all_to_all(partial_value, ('req', 'exp'), split_axis=0, concat_axis=0...  161 us
    all_gather x1, waiting for transfers between devices, body(): lax.all_gather(cache_keys, 'req', axis=0, tiled=True)  152 us
    all_to_all x1, waiting for transfers between devices, body(): lax.all_to_all(copies, ('req', 'exp'), split_axis=0, concat_axis=0, tiled...  145 us
    all_gather x1, waiting for transfers between devices, body(): lax.all_gather(cache_values, 'req', axis=0, tiled=True)  141 us
    reduce_scatter x1, waiting for transfers between devices, body(): lax.psum_scatter(jnp.dot(attended, out_proj, preferred_element_type=jnp.f...  52.4 us
    slice x3, local copies, waits for them, and re-layouts, run_slots(): in_rows = grouped[:, slot_num].reshape(sources * capacity, model_width)  28.2 us
    another operation x2, local copies, waits for them, and re-layouts, run_slots(): in_rows = grouped[:, slot_num].reshape(sources * capacity, model_width)  20.2 us
  transfers between devices with their start and end apart: 7, of which 5 were waited for; matrix products, arithmetic and copies ran while one was open for 19% of the time, Pallas kernels for 0%

commit v1 on v0

--- a/solution.py
+++ b/solution.py
@@ -104,7 +104,9 @@
     need_blocks, need_requests = compact(block_rows, cache_dev)
     my_requests = lax.dynamic_index_in_dim(need_requests, group_idx, 0, keepdims=False)
     every_keys, every_values = (
-        lax.all_gather(cache_keys, "req", axis=0, tiled=True),
+        jnp.concatenate(
+            lax.all_to_all(jnp.stack([cache_keys] * lax.axis_size("req")), "req", 0, 0), axis=0
+        ),
         lax.all_gather(cache_values, "req", axis=0, tiled=True),
     )
     wanted = lax.dynamic_index_in_dim(need_blocks, group_idx, 0, keepdims=False)

time: 928 us -> 774 us (0.83)
  waiting for transfers between devices: 653 us -> 488 us
  starting transfers between devices: 35.8 us -> 45.6 us
    all_gather x1 -> x0, waiting for transfers between devices: 152 us -> none  [body(): lax.all_gather(cache_keys, 'req', axis=0, tiled=True)]
    all_gather x1, waiting for transfers between devices: 141 us -> 111 us  [body(): lax.all_gather(cache_values, 'req', axis=0, tiled=True)]
    all_to_all x0 -> x1, waiting for transfers between devices: none -> 18.4 us  [body(): lax.all_to_all(jnp.stack([cache_keys] * lax.axis_size('req')), 'req', 0, 0)]
  transfers between devices with their start and end apart: 7 -> 7, of which waited for: 5 -> 5; matrix products, arithmetic and copies ran while one was open for 19% -> 23% of each run, Pallas kernels for 0% -> 0%
where the time goes in v1:
time: 774 us; the launch traced here: 763 us
  waiting for transfers between devices  488 us (63%)
  local copies, waits for them, and re-layouts  147 us (19%)
  starting transfers between devices  45.6 us (6%)
  other arithmetic  36 us (5%)
  matrix products  31.5 us (4%)
  between operations  14.9 us (2%)
    all_to_all x1, waiting for transfers between devices, body(): lax.all_to_all(partial_value, ('req', 'exp'), split_axis=0, concat_axis=0...  161 us
    all_to_all x1, waiting for transfers between devices, body(): lax.all_to_all(copies, ('req', 'exp'), split_axis=0, concat_axis=0, tiled...  145 us
    all_gather x1, waiting for transfers between devices, body(): lax.all_gather(cache_values, 'req', axis=0, tiled=True)  111 us
    reduce_scatter x1, waiting for transfers between devices, body(): lax.psum_scatter(jnp.dot(attended, out_proj, preferred_element_type=jnp.f...  52.5 us
    slice x3, local copies, waits for them, and re-layouts, run_slots(): in_rows = grouped[:, slot_num].reshape(sources * capacity, model_width)  28.2 us
    another operation x2, local copies, waits for them, and re-layouts, run_slots(): in_rows = grouped[:, slot_num].reshape(sources * capacity, model_width)  20.2 us
    all_to_all x1, waiting for transfers between devices, body(): lax.all_to_all(jnp.stack([cache_keys] * lax.axis_size('req')), 'req', 0, 0)  18.4 us
  transfers between devices with their start and end apart: 7, of which 5 were waited for; matrix products, arithmetic and copies ran while one was open for 23% of the time, Pallas kernels for 0%

profile of v1, /device:TPU:74, one launch (start us, length us, event | category | flops | bytes accessed | tf_op | source)
XLA Modules:
  0.0 763.2 jit_solution(3486110538960904755)
XLA Ops:
  10.4 8.7 %all-to-all-start = ((bf16[32,2,32,512]{3,2,1,0:T(8,128)(2,1)}), bf16[32,2,32,512]{3,2,1,0:T(8,128)(2,1)}, u32[]{:S(2)}, u32[]{:S(2)}) async-start(bf16[32,2,32,512]{3,2,1,0:T(8,128)(2,1)} %stack.23), calls=%async_computation | async-start | bytes 4194304 | tf_op jit(solution)/shard_map/all_to_all | solution.py:108
  22.4 10.5 %copy.102 = bf16[2,3,2048,256]{3,1,0,2:T(4,128)(2,1)} copy(bf16[2,3,2048,256]{3,2,1,0:T(8,128)(2,1)} %param.35) | data formatting | bytes 12582912 | tf_op args[16]
  35.2 18.4 %all-to-all-done = bf16[32,2,32,512]{3,2,1,0:T(8,128)(2,1)} async-done(((bf16[32,2,32,512]{3,2,1,0:T(8,128)(2,1)}), bf16[32,2,32,512]{3,2,1,0:T(8,128)(2,1)}, u32[]{:S(2)}, u32[]{:S(2)}) %all-to-all-start) | async-done | bytes 2097184 | tf_op jit(solution)/shard_map/all_to_all | solution.py:108
  53.5 9.9 %all-to-all-start.3 = ((bf16[2,3,2048,256]{3,1,0,2:T(4,128)(2,1)}), bf16[2,3,2048,256]{3,1,0,2:T(4,128)(2,1)}, u32[]{:S(2)}, u32[]{:S(2)}) async-start(bf16[2,3,2048,256]{3,1,0,2:T(4,128)(2,1)} %copy.102), calls=%async_computation.4 | async-start | bytes 16777216 | tf_op jit(solution)/shard_map/all_to_all | solution.py:187
  65.6 110.9 %all-gather.2.cloned.1.call-done = bf16[64,32,512]{2,1,0:T(8,128)(2,1)} async-done(((bf16[2,32,512]{2,1,0:T(8,128)(2,1)}), bf16[64,32,512]{2,1,0:T(8,128)(2,1)}) %all-gather.2.cloned.1.call-update) | async-done | bytes 2097168 | tf_op jit(solution)/shard_map/all_gather | solution.py:110
  187.4 52.5 %reduce-scatter.2.cloned.1.call-done = f32[64,2048]{1,0:T(8,128)} async-done(((f32[256,2048]{1,0:T(8,128)}), f32[64,2048]{1,0:T(8,128)}) %reduce-scatter.2.cloned.1.call-update) | async-done | bytes 524304 | tf_op jit(solution)/shard_map/reduce_scatter | solution.py:138
  242.3 5.6 scatter_custom_fusion
  253.0 8.1 %broadcast_in_dim.196 = bf16[32,4,20,2048]{3,2,1,0:T(8,128)(2,1)} broadcast(bf16[32,20,2048]{2,1,0:T(8,128)(2,1)} %broadcast_in_dim.195), dimensions={0,2,3} | broadcast | bytes 13107200 | tf_op jit(solution)/shard_map/broadcast_in_dim | solution.py:167
  261.1 9.2 %all-to-all-start.1 = ((bf16[128,20,2048]{2,1,0:T(8,128)(2,1)}), bf16[128,20,2048]{2,1,0:T(8,128)(2,1)}, u32[]{:S(2)}, u32[]{:S(2)}) async-start(bf16[128,20,2048]{2,1,0:T(8,128)(2,1)} %bitcast.109), calls=%async_computation.2 | async-start | bytes 25165824 | tf_op jit(solution)/shard_map/all_to_all | solution.py:171
  287.8 145.0 %all-to-all-done.1 = bf16[128,20,2048]{2,1,0:T(8,128)(2,1)} async-done(((bf16[128,20,2048]{2,1,0:T(8,128)(2,1)}), bf16[128,20,2048]{2,1,0:T(8,128)(2,1)}, u32[]{:S(2)}, u32[]{:S(2)}) %all-to-all-start.1) | async-done | bytes 10485792 | tf_op jit(solution)/shard_map/all_to_all | solution.py:171
  432.9 6.8 all-to-all-start.4
  439.7 12.6 %copy.93 = bf16[128,20,2048]{2,0,1:T(8,128)(2,1)} copy(bf16[128,20,2048]{2,1,0:T(8,128)(2,1)} %all-to-all-done.1) | data formatting | bytes 20971520 | tf_op jit(solution)/shard_map/all_to_all | solution.py:171
  452.3 10.2 %fusion.64 = (bf16[128,1,10,2048]{3,0,2,1:T(8,128)(2,1)}, bf16[128,1,10,2048]{3,0,2,1:T(8,128)(2,1)}) fusion(bf16[128,2,10,2048]{3,0,2,1:T(8,128)(2,1)} %bitcast.110), kind=kLoop, calls=%fused_computation.135 | loop fusion | bytes 20971520 | tf_op jit(solution)/shard_map/slice | solution.py:48
  462.5 9.0 %copy.94 = bf16[128,1,10,2048]{3,2,0,1:T(8,128)(2,1)} copy(bf16[128,1,10,2048]{3,0,2,1:T(8,128)(2,1)} %get-tuple-element.14) | data formatting | bytes 10485760 | tf_op jit(solution)/shard_map/slice | solution.py:48
  471.5 10.0 %reshape_squeeze.6 = bf16[1280,2048]{1,0:T(8,128)(2,1)} reshape(bf16[128,1,10,2048]{3,2,0,1:T(8,128)(2,1)} %copy.94) | data formatting | bytes 10485760 | tf_op jit(solution)/shard_map/reshape;squeeze | solution.py:48
  489.2 9.0 %copy.96 = bf16[128,1,10,2048]{3,2,0,1:T(8,128)(2,1)} copy(bf16[128,1,10,2048]{3,0,2,1:T(8,128)(2,1)} %get-tuple-element.15) | data formatting | bytes 10485760 | tf_op jit(solution)/shard_map/slice | solution.py:48
  498.2 10.2 %reshape_squeeze.7 = bf16[1280,2048]{1,0:T(8,128)(2,1)} reshape(bf16[128,1,10,2048]{3,2,0,1:T(8,128)(2,1)} %copy.96) | data formatting | bytes 10485760 | tf_op jit(solution)/shard_map/reshape;squeeze | solution.py:48
  526.3 9.0 %pad_maximum_fusion = bf16[128,2,10,2048]{3,0,2,1:T(8,128)(2,1)} fusion(bf16[128,1,10,2048]{3,0,2,1:T(8,128)(2,1)} %convert_bitcast_fusion, bf16[128,1,10,2048]{3,0,2,1:T(8,128)(2,1)} %convert_bitcast_fusion.1), kind=kLoop, calls=%fused_computation.7 | loop fusion | flops 5242880 | bytes 20971520 | tf_op jit(solution)/shard_map/stack | solution.py:59
  535.3 14.1 %copy.98 = bf16[128,20,2048]{2,1,0:T(8,128)(2,1)} copy(bf16[128,20,2048]{2,0,1:T(8,128)(2,1)} %bitcast.111) | data formatting | bytes 20971520 | tf_op jit(solution)/shard_map/convert_element_type | solution.py:172
  549.4 10.9 %all-to-all-start.2 = ((bf16[128,20,2048]{2,1,0:T(8,128)(2,1)}), bf16[128,20,2048]{2,1,0:T(8,128)(2,1)}, u32[]{:S(2)}, u32[]{:S(2)}) async-start(bf16[128,20,2048]{2,1,0:T(8,128)(2,1)} %copy.98), calls=%async_computation.3 | async-start | bytes 25165824 | tf_op jit(solution)/shard_map/all_to_all | solution.py:173
  564.4 160.7 %all-to-all-done.2 = bf16[128,20,2048]{2,1,0:T(8,128)(2,1)} async-done(((bf16[128,20,2048]{2,1,0:T(8,128)(2,1)}), bf16[128,20,2048]{2,1,0:T(8,128)(2,1)}, u32[]{:S(2)}, u32[]{:S(2)}) %all-to-all-start.2) | async-done | bytes 10485792 | tf_op jit(solution)/shard_map/all_to_all | solution.py:173
  725.2 11.1 %convert_reduce_fusion = f32[32,20,2048]{2,1,0:T(8,128)} fusion(bf16[128,20,2048]{2,1,0:T(8,128)(2,1)} %all-to-all-done.2), kind=kLoop, calls=%fused_computation.6 | loop fusion | flops 9175040 | bytes 15728640 | tf_op jit(solution)/shard_map/reduce_sum | solution.py:176
  736.3 6.8 reshape.303
  743.1 8.1 %gather_fusion = f32[512,2048]{1,0:T(8,128)} fusion(f32[640,2048]{1,0:T(8,128)} %reshape.303, s32[1024]{0:T(1024)S(1)} %pad_clamp_fusion.1), kind=kCustom, calls=%fused_computation.2 | custom fusion | bytes 8390656 | tf_op jit(solution)/shard_map/jit(_take)/gather | solution.py:182
  (129 shorter events, 80.9 us)
Async XLA Ops:
  7.2 176.1 %copy-start = (bf16[512,2048]{1,0:T(8,128)(2,1)S(1)}, bf16[512,2048]{1,0:T(8,128)(2,1)}, u32[]{:S(2)}) copy-start(bf16[512,2048]{1,0:T(8,128)(2,1)} %param.29) | copy-start | bytes 6291460
  7.2 12.0 %copy-start.13 = (s32[128]{0:T(128)S(1)}, s32[128]{0:T(128)}, u32[]{:S(2)}) copy-start(s32[128]{0:T(128)} %param.27) | copy-start | bytes 1540
  7.2 13.0 %copy-start.16 = (s32[1,4]{1,0:T(1,128)S(1)}, s32[1,4]{1,0:T(1,128)}, u32[]{:S(2)}) copy-start(s32[1,4]{1,0:T(1,128)} %param.28) | copy-start | bytes 52
  7.2 13.2 %copy-start.7 = (bf16[256,512]{1,0:T(8,128)(2,1)S(1)}, bf16[256,512]{1,0:T(8,128)(2,1)}, u32[]{:S(2)}) copy-start(bf16[256,512]{1,0:T(8,128)(2,1)} %param.20) | copy-start | bytes 786436
  7.2 13.3 %copy-start.8 = (bf16[256,512]{1,0:T(8,128)(2,1)S(1)}, bf16[256,512]{1,0:T(8,128)(2,1)}, u32[]{:S(2)}) copy-start(bf16[256,512]{1,0:T(8,128)(2,1)} %param.21) | copy-start | bytes 786436
  7.2 169.3 %all-gather.2.cloned.1.call-start = ((), (), s32[]{:S(2)}) async-start(), calls=%async_computation.6 | async-start | bytes 2162688 | tf_op jit(solution)/shard_map/all_gather | solution.py:110
  10.4 11.6 %copy-start.9 = (bf16[256,512]{1,0:T(8,128)(2,1)S(1)}, bf16[256,512]{1,0:T(8,128)(2,1)}, u32[]{:S(2)}) copy-start(bf16[256,512]{1,0:T(8,128)(2,1)} %param.22) | copy-start | bytes 786436
  10.4 43.1 %all-to-all-start = ((bf16[32,2,32,512]{3,2,1,0:T(8,128)(2,1)}), bf16[32,2,32,512]{3,2,1,0:T(8,128)(2,1)}, u32[]{:S(2)}, u32[]{:S(2)}) async-start(bf16[32,2,32,512]{3,2,1,0:T(8,128)(2,1)} %stack.23), calls=%async_computation | async-start | bytes 4194304 | tf_op jit(solution)/shard_map/all_to_all | solution.py:108
  22.3 11.3 %copy-start.6 = (f32[256,4,128]{2,0,1:T(8,128)S(1)}, f32[256,4,128]{2,0,1:T(8,128)}, u32[]{:S(2)}) copy-start(f32[256,4,128]{2,0,1:T(8,128)} %copy.88) | copy-start | bytes 1572868
  22.4 11.3 %copy-start.14 = (f32[128]{0:T(128)S(1)}, f32[128]{0:T(128)}, u32[]{:S(2)}) copy-start(f32[128]{0:T(128)} %param.24) | copy-start | bytes 1540
  22.4 11.3 %copy-start.15 = (f32[128]{0:T(128)S(1)}, f32[128]{0:T(128)}, u32[]{:S(2)}) copy-start(f32[128]{0:T(128)} %param.23) | copy-start | bytes 1540
  53.5 199.5 %all-to-all-start.3 = ((bf16[2,3,2048,256]{3,1,0,2:T(4,128)(2,1)}), bf16[2,3,2048,256]{3,1,0,2:T(4,128)(2,1)}, u32[]{:S(2)}, u32[]{:S(2)}) async-start(bf16[2,3,2048,256]{3,1,0,2:T(4,128)(2,1)} %copy.102), calls=%async_computation.4 | async-start | bytes 16777216 | tf_op jit(solution)/shard_map/all_to_all | solution.py:187
  63.4 176.5 %reduce-scatter.2.cloned.1.call-start = ((), (), s32[]{:S(2)}) async-start(), calls=%async_computation.7 | async-start | bytes 2621440 | tf_op jit(solution)/shard_map/reduce_scatter | solution.py:138
  183.2 56.7 %copy-start.5 = (bf16[64,2048]{1,0:T(8,128)(2,1)S(1)}, bf16[64,2048]{1,0:T(8,128)(2,1)}, u32[]{:S(2)}) copy-start(bf16[64,2048]{1,0:T(8,128)(2,1)} %param.19) | copy-start | bytes 786436
  183.2 57.9 %copy-start.10 = (f32[2048]{0:T(1024)S(1)}, f32[2048]{0:T(1024)}, u32[]{:S(2)}) copy-start(f32[2048]{0:T(1024)} %param.30) | copy-start | bytes 24580
  261.1 9.2 %copy-start.18 = (s32[32]{0:T(128)S(1)}, s32[32]{0:T(128)}, u32[]{:S(2)}) copy-start(s32[32]{0:T(128)} %param.34) | copy-start | bytes 388
  261.1 171.7 %all-to-all-start.1 = ((bf16[128,20,2048]{2,1,0:T(8,128)(2,1)}), bf16[128,20,2048]{2,1,0:T(8,128)(2,1)}, u32[]{:S(2)}, u32[]{:S(2)}) async-start(bf16[128,20,2048]{2,1,0:T(8,128)(2,1)} %bitcast.109), calls=%async_computation.2 | async-start | bytes 25165824 | tf_op jit(solution)/shard_map/all_to_all | solution.py:171
  432.9 116.5 %all-to-all-start.4 = ((bf16[32,3,64,256]{3,2,1,0:T(8,128)(2,1)}), bf16[32,3,64,256]{3,2,1,0:T(8,128)(2,1)}, u32[]{:S(2)}, u32[]{:S(2)}) async-start(bf16[32,3,64,256]{3,2,1,0:T(8,128)(2,1)} %broadcast_select_fusion), calls=%async_computation.5 | async-start | bytes 6291456 | tf_op jit(solution)/shard_map/all_to_all | solution.py:191
  481.5 4.5 copy-start.2
  508.5 4.5 copy-start.3
  549.4 11.0 %copy-start.12 = (f32[64,8]{0,1:T(8,128)S(1)}, f32[64,8]{0,1:T(8,128)}, u32[]{:S(2)}) copy-start(f32[64,8]{0,1:T(8,128)} %param.32) | copy-start | bytes 6148
  549.4 175.8 %all-to-all-start.2 = ((bf16[128,20,2048]{2,1,0:T(8,128)(2,1)}), bf16[128,20,2048]{2,1,0:T(8,128)(2,1)}, u32[]{:S(2)}, u32[]{:S(2)}) async-start(bf16[128,20,2048]{2,1,0:T(8,128)(2,1)} %copy.98), calls=%async_computation.3 | async-start | bytes 25165824 | tf_op jit(solution)/shard_map/all_to_all | solution.py:173
  743.1 13.0 %copy-start.1 = (bf16[512,2048]{1,0:T(8,128)(2,1)S(1)}, bf16[512,2048]{1,0:T(8,128)(2,1)}, u32[]{:S(2)}) copy-start(bf16[512,2048]{1,0:T(8,128)(2,1)} %param.29) | copy-start | bytes 6291460
  751.2 4.1 copy-start.4
  (2 other events, 6.0 us)
Sparse Core Ops, SparseCore 0:
  9.7 166.7 all-gather.1
  185.5 54.3 reduce-scatter.1
